TPU v7x, 256 devices: a whole 4x4x8 slice. The times are simulated.
256 devices in a mesh: dp: 16 (over x, y), tensor: 16 (over z, core).
Axes of the slice: x: 4, y: 4, z: 8, core: 2. Of those that a mesh axis runs over, the one named last changes fastest.
Arguments:
- out_grad: bfloat16 [12288, 8192], P('dp', 'tensor'), may hold values from -6 to 6
- block_input: bfloat16 [12288, 8192], P('dp', 'tensor'), may hold values from -6 to 6
- gate_pre: bfloat16 [12288, 14336], P('dp', 'tensor'), may hold values from -8 to 8
- up_pre: bfloat16 [12288, 14336], P('dp', 'tensor'), may hold values from -6 to 6
- down_weight: bfloat16 [14336, 8192], P('tensor', 'dp'), may hold values from -0.046875 to 0.046875
- gate_in: bfloat16 [48, 16, 8192], P(None, None, 'tensor'), may hold values from -0.0625 to 0.0625
- gate_adapter_output_maps: bfloat16 [48, 16, 14336], P(None, None, 'tensor'), may hold values from -0.046875 to 0.046875
- up_in: bfloat16 [48, 16, 8192], P(None, None, 'tensor'), may hold values from -0.0625 to 0.0625
- up_adapter_output_maps: bfloat16 [48, 16, 14336], P(None, None, 'tensor'), may hold values from -0.046875 to 0.046875
- down_in: bfloat16 [48, 16, 14336], P(None, None, 'tensor'), may hold values from -0.046875 to 0.046875
- down_out: bfloat16 [48, 16, 8192], P(None, None, 'tensor'), may hold values from -0.0625 to 0.0625
- block_adapter: int32 [96], replicated, may hold values from 0 to 47, as said below
- owned_ids: int32 [48], replicated, may hold values from 0 to 47, as said below
Outputs:
- input_grad: bfloat16 [12288, 8192], P('dp', 'tensor')
- grad_gate_in: float32 [48, 16, 8192], P('dp', None, 'tensor')
- grad_gate_out: float32 [48, 16, 14336], P('dp', None, 'tensor')
- grad_up_in: float32 [48, 16, 8192], P('dp', None, 'tensor')
- grad_up_out: float32 [48, 16, 14336], P('dp', None, 'tensor')
- grad_down_in: float32 [48, 16, 14336], P('dp', None, 'tensor')
- grad_down_out: float32 [48, 16, 8192], P('dp', None, 'tensor')
Inputs may be any that keep to these rules, and one draw needn't show every extreme that they name: `block_adapter`: replica q (blocks q * 6 to q * 6 + 5) owns the adapters owned_ids[q * 3] to owned_ids[q * 3 + 2]. Among the 6 blocks of one replica, at most 1 names an adapter of any one owner; in every draw each replica has some owner that it names exactly once. `owned_ids`: each adapter appears once.
All inputs are finite; a program needn't handle non-finite values.
Results may differ from a plain program's by a relative error of at most 0.0058.
Values may be sent and summed in bfloat16 or wider, within the bound.
A program may use at most 128 MiB of HBM per device.

v0:
```python
import jax
import jax.numpy as jnp
from jax import lax
from jax.sharding import PartitionSpec as P

adapter_scale_factor = 2.0


def apply_projection(left, table):
    return jnp.einsum("nbd,nrd->nrb", left, table, preferred_element_type=jnp.float32)


def outer_product_sum(low, right):
    return jnp.einsum("nrb,nbw->nrw", low, right, preferred_element_type=jnp.float32)


def shards(
    out_grad,
    block_input,
    gate_pre,
    up_pre,
    down_weight,
    gate_in,
    gate_adapter_output_maps,
    up_in,
    up_adapter_output_maps,
    down_in,
    down_out,
    block_adapter,
    owned_ids,
):
    replicas = lax.axis_size("dp")
    replica = lax.axis_index("dp")
    tok_rows, width_part = out_grad.shape
    hidden_width_slice = gate_pre.shape[1]
    blocks_all = block_adapter.reshape(replicas, -1)
    block_count = blocks_all.shape[1]
    rows_per_block = tok_rows // block_count
    adapters = owned_ids.shape[0]
    owned = adapters // replicas
    capacity = (block_count + replicas - 1) // replicas
    my_ids = lax.dynamic_index_in_dim(blocks_all, replica, 0, keepdims=False)
    g_in = jnp.take(gate_in, my_ids, axis=0)
    gate_output_grad = jnp.take(gate_adapter_output_maps, my_ids, axis=0)
    u_in = jnp.take(up_in, my_ids, axis=0)
    up_output_grad = jnp.take(up_adapter_output_maps, my_ids, axis=0)
    input_dimension = jnp.take(down_in, my_ids, axis=0)
    d_out = jnp.take(down_out, my_ids, axis=0)
    output_grad_blocks = out_grad.reshape(block_count, rows_per_block, width_part)
    input_blocks = block_input.reshape(block_count, rows_per_block, width_part)
    gate_f = gate_pre.reshape(block_count, rows_per_block, hidden_width_slice).astype(jnp.float32)
    up_f = up_pre.reshape(block_count, rows_per_block, hidden_width_slice).astype(jnp.float32)
    hidden_activation = (jax.nn.silu(gate_f) * up_f).astype(jnp.bfloat16)
    partials = (
        apply_projection(input_blocks, g_in),
        apply_projection(input_blocks, u_in),
        apply_projection(hidden_activation, input_dimension),
        apply_projection(output_grad_blocks, d_out),
    )
    reduced = lax.psum((partials[0], partials[1], partials[2], partials[3]), "tensor")
    rank_gate_projection = reduced[0].astype(jnp.bfloat16)
    rank_up_projection = reduced[1].astype(jnp.bfloat16)
    rank_down_projection = reduced[2].astype(jnp.bfloat16)
    down_error_signal = reduced[3].astype(jnp.bfloat16)
    dy_full = lax.all_gather(out_grad, "tensor", axis=1, tiled=True)
    frozen_base_output = lax.dot_general(
        dy_full,
        lax.all_gather(down_weight, "dp", axis=1, tiled=True),
        (((1,), (1,)), ((), ())),
        preferred_element_type=jnp.float32,
    )
    hidden_gradient_rows = frozen_base_output.reshape(
        block_count, rows_per_block, hidden_width_slice
    ) + adapter_scale_factor * jnp.einsum(
        "elz,elp->ezp", down_error_signal, input_dimension, preferred_element_type=jnp.float32
    )
    sigmoid_gate = jax.nn.sigmoid(gate_f)
    gate_gradient_total = (
        hidden_gradient_rows * up_f * sigmoid_gate * (1.0 + gate_f * (1.0 - sigmoid_gate))
    ).astype(jnp.bfloat16)
    up_gradient_total = (hidden_gradient_rows * gate_f * sigmoid_gate).astype(jnp.bfloat16)
    returned = lax.psum(
        (
            adapter_scale_factor * apply_projection(gate_gradient_total, gate_output_grad),
            adapter_scale_factor * apply_projection(up_gradient_total, up_output_grad),
        ),
        "tensor",
    )
    gate_backward = returned[0].astype(jnp.bfloat16)
    up_backward = returned[1].astype(jnp.bfloat16)
    input_grad = jnp.einsum(
        "nrb,nrd->nbd", gate_backward, g_in, preferred_element_type=jnp.float32
    ) + jnp.einsum("nrb,nrd->nbd", up_backward, u_in, preferred_element_type=jnp.float32)
    input_grad = input_grad.astype(jnp.bfloat16).reshape(tok_rows, width_part)
    packet = jnp.concatenate(
        [
            outer_product_sum(gate_backward, input_blocks),
            adapter_scale_factor * outer_product_sum(rank_gate_projection, gate_gradient_total),
            outer_product_sum(up_backward, input_blocks),
            adapter_scale_factor * outer_product_sum(rank_up_projection, up_gradient_total),
            adapter_scale_factor * outer_product_sum(down_error_signal, hidden_activation),
            adapter_scale_factor * outer_product_sum(rank_down_projection, output_grad_blocks),
        ],
        axis=2,
    )
    order_index = jnp.arange(adapters, dtype=jnp.int32)
    rank_of = jnp.sum(
        jnp.where(owned_ids[None, :] == order_index[:, None], order_index[None, :], 0), axis=1
    )
    position = jnp.take(rank_of, blocks_all)
    target_all = position // owned
    local_all = position % owned
    block_index = jnp.arange(block_count, dtype=jnp.int32)
    earlier = block_index[:, None] > block_index[None, :]
    same_target = target_all[:, :, None] == target_all[:, None, :]
    slot_all = jnp.sum(jnp.logical_and(same_target, earlier[None, :, :]).astype(jnp.int32), axis=2)
    my_target = lax.dynamic_index_in_dim(target_all, replica, 0, keepdims=False)
    my_slot = lax.dynamic_index_in_dim(slot_all, replica, 0, keepdims=False)
    replica_index = jnp.arange(replicas, dtype=jnp.int32)
    slot_index = jnp.arange(capacity, dtype=jnp.int32)
    owned_index = jnp.arange(owned, dtype=jnp.int32)
    send_table = jnp.logical_and(
        my_target[None, None, :] == replica_index[:, None, None],
        my_slot[None, None, :] == slot_index[None, :, None],
    ).astype(jnp.float32)
    outgoing = jnp.einsum("qcn,nrw->qcrw", send_table, packet, precision=lax.Precision.HIGHEST)
    mine = (target_all == replica)[:, None, :, None]
    slot_match = slot_all[:, None, :, None] == slot_index[None, :, None, None]
    local_match = local_all[:, None, :, None] == owned_index[None, None, None, :]
    receive_table = jnp.sum(
        jnp.logical_and(jnp.logical_and(mine, slot_match), local_match).astype(jnp.float32), axis=2
    )
    owned_grads = jnp.einsum(
        "qco,qckw->okw",
        receive_table,
        lax.all_to_all(
            outgoing.astype(jnp.bfloat16), "dp", split_axis=0, concat_axis=0, tiled=True
        ).astype(outgoing.dtype),
        precision=lax.Precision.HIGHEST,
    )
    second = width_part + hidden_width_slice
    third = second + width_part
    fourth = third + hidden_width_slice
    fifth = fourth + hidden_width_slice
    return (
        input_grad,
        owned_grads[:, :, :width_part],
        owned_grads[:, :, width_part:second],
        owned_grads[:, :, second:third],
        owned_grads[:, :, third:fourth],
        owned_grads[:, :, fourth:fifth],
        owned_grads[:, :, fifth:],
    )


def solution(mesh):
    in_specs = (
        P("dp", "tensor"),
        P("dp", "tensor"),
        P("dp", "tensor"),
        P("dp", "tensor"),
        P("tensor", "dp"),
        P(None, None, "tensor"),
        P(None, None, "tensor"),
        P(None, None, "tensor"),
        P(None, None, "tensor"),
        P(None, None, "tensor"),
        P(None, None, "tensor"),
        P(),
        P(),
    )
    out_specs = (
        P("dp", "tensor"),
        P("dp", None, "tensor"),
        P("dp", None, "tensor"),
        P("dp", None, "tensor"),
        P("dp", None, "tensor"),
        P("dp", None, "tensor"),
        P("dp", None, "tensor"),
    )
    return jax.shard_map(shards, mesh=mesh, in_specs=in_specs, out_specs=out_specs, check_vma=False)
```

profile of v0, /device:TPU:112, one launch (start us, length us, event | category | flops | bytes accessed | tf_op | source)
XLA Modules:
  0.0 331.0 jit_solution(10830039742640613778)
XLA Ops:
  9.2 1.2 gather_fusion
  11.4 1.7 gather_fusion.6
  13.4 1.7 gather_fusion.4
  15.1 1.0 fusion.30
  16.1 2.3 gather_fusion.2
  18.5 1.2 gather_fusion.3
  19.7 1.9 gather_fusion.5
  21.6 1.9 gather_fusion.1
  24.4 1.2 fusion.23
  25.6 50.8 %psum.42 = bf16[6,16,128]{2,1,0:T(8,128)(2,1)S(1)} all-reduce(f32[6,16,128]{2,1,0:T(8,128)S(1)} %fusion.23), channel_id=1, replica_groups=mesh['dp'=16,'tensor'=16] {'tensor'}, use_global_device_ids=true, to_apply=%region_0.0 | all-reduce | flops 12288 | bytes 73728 | tf_op jit(solution)/shard_map/psum | solution.py:60
  76.4 10.7 %all-gather.3.cloned.1.call-done = bf16[768,8192]{1,0:T(8,128)(2,1)} async-done(((bf16[768,512]{1,0:T(8,128)(2,1)}), bf16[768,8192]{1,0:T(8,128)(2,1)}) %all-gather.3.cloned.1.call-update) | async-done | bytes 12582928 | tf_op jit(solution)/shard_map/all_gather | solution.py:65
  87.2 114.3 %all-gather.5.cloned.1.call-done = bf16[896,8192]{1,0:T(8,128)(2,1)} async-done(((bf16[896,512]{1,0:T(8,128)(2,1)}), bf16[896,8192]{1,0:T(8,128)(2,1)}) %all-gather.5.cloned.1.call-update) | async-done | bytes 14680080 | tf_op jit(solution)/shard_map/all_gather | solution.py:68
  201.5 17.9 %fusion.63 = f32[768,896]{1,0:T(8,128)S(1)} fusion(bf16[768,8192]{1,0:T(8,128)(2,1)} %all-gather.3.cloned.1.call-done, bf16[896,8192]{1,0:T(8,128)(2,1)} %all-gather.5.cloned.1.call-done), kind=kOutput, calls=%fused_computation.110 | convolution fusion | flops 11274289152 | bytes 30015488 | tf_op jit(solution)/shard_map/dot_general | solution.py:66
  219.5 2.2 fusion.10
  221.7 1.1 copy-done.3
  224.5 47.3 %all-reduce.2 = (bf16[6,16,128]{2,1,0:T(8,128)(2,1)S(1)}, bf16[6,16,128]{2,1,0:T(8,128)(2,1)S(1)}, bf16[6,16,128]{2,1,0:T(8,128)(2,1)S(1)}, bf16[6,16,128]{2,1,0:T(8,128)(2,1)S(1)}, bf16[6,16,128]{2,1,0:T(8,128)(2,1)S(1)}) all-reduce(f32[6,16,128]{2,1,0:T(8,128)S(1)} %convolution_multiply_fusion.5,, ...), channel_id=1, replica_groups=mesh['dp'=16,'tensor'=16] {'tensor'}, use_global_device_ids=true, to_apply=%region_1.4 | all-reduce | flops 61440 | bytes 368640 | tf_op jit(solution)/shard_map/psum | solution.py:82
  272.4 1.7 fusion.17
  276.1 2.6 fusion
  278.8 1.7 copy.59
  280.5 6.9 %all-to-all-start = ((bf16[16,1,16,4224]{3,2,1,0:T(8,128)(2,1)}), bf16[16,1,16,4224]{3,2,1,0:T(8,128)(2,1)S(1)}, u32[]{:S(2)}, u32[]{:S(2)}) async-start(bf16[16,1,16,4224]{3,2,1,0:T(8,128)(2,1)} %copy.59), calls=%async_computation | async-start | bytes 4325376 | tf_op jit(solution)/shard_map/all_to_all | solution.py:136
  287.5 1.3 fusion.31
  288.8 1.3 add_convert_fusion
  290.1 28.6 %all-to-all-done = bf16[16,1,16,4224]{3,2,1,0:T(8,128)(2,1)S(1)} async-done(((bf16[16,1,16,4224]{3,2,1,0:T(8,128)(2,1)}), bf16[16,1,16,4224]{3,2,1,0:T(8,128)(2,1)S(1)}, u32[]{:S(2)}, u32[]{:S(2)}) %all-to-all-start) | async-done | bytes 2162720 | tf_op jit(solution)/shard_map/all_to_all | solution.py:136
  318.7 1.1 fusion.11
  (85 shorter events, 12.6 us)
Async XLA Ops:
  7.2 11.3 %copy-start = (bf16[48,16,896]{2,1,0:T(8,128)(2,1)S(1)}, bf16[48,16,896]{2,1,0:T(8,128)(2,1)}, u32[]{:S(2)}) copy-start(bf16[48,16,896]{2,1,0:T(8,128)(2,1)} %param.26) | copy-start | bytes 4128772
  7.2 1.5 copy-start.20
  7.2 1.9 copy-start.23
  7.2 80.0 %all-gather.3.cloned.1.call-start = ((), (), s32[]{:S(2)}) async-start(), calls=%async_computation.1 | async-start | bytes 13369344 | tf_op jit(solution)/shard_map/all_gather | solution.py:65
  7.9 193.5 %all-gather.5.cloned.1.call-start = ((), (), s32[]{:S(2)}) async-start(), calls=%async_computation.2 | async-start | bytes 15597568 | tf_op jit(solution)/shard_map/all_gather | solution.py:68
  9.2 3.8 %copy-start.1 = (bf16[768,512]{1,0:T(8,128)(2,1)S(1)}, bf16[768,512]{1,0:T(8,128)(2,1)}, u32[]{:S(2)}) copy-start(bf16[768,512]{1,0:T(8,128)(2,1)} %param.18) | copy-start | bytes 2359300
  13.0 10.5 %copy-start.8 = (bf16[6,16,512]{2,1,0:T(8,128)(2,1)}, bf16[6,16,512]{2,1,0:T(8,128)(2,1)S(1)}, u32[]{:S(2)}) copy-start(bf16[6,16,512]{2,1,0:T(8,128)(2,1)S(1)} %gather_fusion.6) | copy-start | bytes 294916
  13.1 11.3 %copy-start.2 = (bf16[768,512]{1,0:T(8,128)(2,1)S(1)}, bf16[768,512]{1,0:T(8,128)(2,1)}, u32[]{:S(2)}) copy-start(bf16[768,512]{1,0:T(8,128)(2,1)} %param.17) | copy-start | bytes 2359300
  15.1 204.3 %copy-start.10 = (bf16[6,16,512]{2,1,0:T(8,128)(2,1)}, bf16[6,16,512]{2,1,0:T(8,128)(2,1)S(1)}, u32[]{:S(2)}) copy-start(bf16[6,16,512]{2,1,0:T(8,128)(2,1)S(1)} %gather_fusion.4) | copy-start | bytes 294916
  76.4 143.0 %copy-start.15 = (bf16[6,16,128]{2,1,0:T(8,128)(2,1)}, bf16[6,16,128]{2,1,0:T(8,128)(2,1)S(1)}, u32[]{:S(2)}) copy-start(bf16[6,16,128]{2,1,0:T(8,128)(2,1)S(1)} %psum.42) | copy-start | bytes 73732
  201.5 18.0 %copy-start.11 = (bf16[6,16,896]{2,1,0:T(8,128)(2,1)S(1)}, bf16[6,16,896]{2,1,0:T(8,128)(2,1)}, u32[]{:S(2)}) copy-start(bf16[6,16,896]{2,1,0:T(8,128)(2,1)} %gather_fusion.3) | copy-start | bytes 516100
  201.5 18.0 %copy-start.21 = (bf16[768,896]{1,0:T(8,128)(2,1)S(1)}, bf16[768,896]{1,0:T(8,128)(2,1)}, u32[]{:S(2)}) copy-start(bf16[768,896]{1,0:T(8,128)(2,1)} %param.19) | copy-start | bytes 4128772
  201.5 18.0 %copy-start.22 = (bf16[768,896]{1,0:T(8,128)(2,1)S(1)}, bf16[768,896]{1,0:T(8,128)(2,1)}, u32[]{:S(2)}) copy-start(bf16[768,896]{1,0:T(8,128)(2,1)} %param.20) | copy-start | bytes 4128772
  221.7 1.1 copy-start.3
  221.7 1.6 copy-start.5
  221.7 2.2 copy-start.7
  223.3 1.1 copy-start.12
  271.8 2.5 copy-start.13
  272.0 2.3 copy-start.6
  274.1 1.3 copy-start.4
  274.1 1.4 copy-start.16
  280.5 38.3 %all-to-all-start = ((bf16[16,1,16,4224]{3,2,1,0:T(8,128)(2,1)}), bf16[16,1,16,4224]{3,2,1,0:T(8,128)(2,1)S(1)}, u32[]{:S(2)}, u32[]{:S(2)}) async-start(bf16[16,1,16,4224]{3,2,1,0:T(8,128)(2,1)} %copy.59), calls=%async_computation | async-start | bytes 4325376 | tf_op jit(solution)/shard_map/all_to_all | solution.py:136
  287.4 1.4 copy-start.9
  287.4 1.4 copy-start.14
  (3 other events, 1.9 us)
Sparse Core Ops, SparseCore 0:
  9.9 77.2 all-gather.2
  89.6 111.8 all-gather.4
where the time goes:
time: 331 us
  waiting for transfers between devices  155 us (47%)
  blocking collectives  98.1 us (30%)
  matrix products  33.8 us (10%)
  local copies, waits for them, and re-layouts  21.6 us (7%)
  between operations  14.4 us (4%)
  starting transfers between devices  7.01 us (2%)
    all_gather x1, waiting for transfers between devices, shards(): lax.all_gather(down_weight, 'dp', axis=1, tiled=True)  114 us
    psum x1, blocking collectives, shards(): lax.psum((partials[0], partials[1], partials[2], partials[3]), 'tensor')  50.8 us
    psum x1, blocking collectives, shards(): lax.psum((adapter_scale_factor * apply_projection(gate_gradient_total, ga...  47.3 us
    all_to_all x1, waiting for transfers between devices, shards(): lax.all_to_all(outgoing.astype(jnp.bfloat16), 'dp', split_axis=0, concat_...  28.6 us
    dot_general x1, matrix products, shards(): lax.dot_general(dy_full, lax.all_gather(down_weight, 'dp', axis=1, tiled=...  17.9 us
    all_gather x1, waiting for transfers between devices, shards(): dy_full = lax.all_gather(out_grad, 'tensor', axis=1, tiled=True)  10.7 us
    all_to_all x1, starting transfers between devices, shards(): lax.all_to_all(outgoing.astype(jnp.bfloat16), 'dp', split_axis=0, concat_...  6.93 us
  transfers between devices with their start and end apart: 3, of which 3 were waited for; matrix products, arithmetic and copies ran while one was open for 6% of the time, Pallas kernels for 0%

commit v1 on v0

--- a/solution.py
+++ b/solution.py
@@ -2,8 +2,12 @@
 import jax.numpy as jnp
 from jax import lax
 from jax.sharding import PartitionSpec as P
+from jax.lax import all_to_all, axis_size
 
 adapter_scale_factor = 2.0
+_link_page = lambda arr, across: jnp.concatenate(
+    all_to_all(jnp.stack([arr for _ in range(axis_size(across))], axis=0), across, 0, 0), axis=1
+)
 
 
 def apply_projection(left, table):
@@ -65,7 +69,7 @@
     dy_full = lax.all_gather(out_grad, "tensor", axis=1, tiled=True)
     frozen_base_output = lax.dot_general(
         dy_full,
-        lax.all_gather(down_weight, "dp", axis=1, tiled=True),
+        _link_page(down_weight, "dp"),
         (((1,), (1,)), ((), ())),
         preferred_element_type=jnp.float32,
     )

time: 331 us -> 457 us (1.38)
  local copies, waits for them, and re-layouts: 21.6 us -> 66.3 us
  waiting for transfers between devices: 155 us -> 198 us
  starting transfers between devices: 7.01 us -> 36.8 us
  matrix products: 33.8 us -> 41.5 us
    all_to_all x0 -> x1, waiting for transfers between devices: none -> 168 us  [all_to_all(jnp.stack([arr for _ in range(axis_size(across))], axis=0), ac...]
    all_gather x1 -> x0, waiting for transfers between devices: 114 us -> none  [shards(): lax.all_gather(down_weight, 'dp', axis=1, tiled=True)]
    reshape x0 -> x2, local copies, waits for them, and re-layouts: none -> 39 us  [jnp.concatenate(all_to_all(jnp.stack([arr for _ in range(axis_size(across...]
    all_to_all x1, starting transfers between devices: 6.93 us -> 29.3 us  [shards(): lax.all_to_all(outgoing.astype(jnp.bfloat16), 'dp', split_axis=0, concat_...]
    all_gather x1, waiting for transfers between devices: 10.7 us -> 0.01 us  [shards(): dy_full = lax.all_gather(out_grad, 'tensor', axis=1, tiled=True)]
    another operation x0 -> x1, local copies, waits for them, and re-layouts: none -> 7.74 us  [jnp.stack([arr for _ in range(axis_size(across))], axis=0)]
    all_to_all x0 -> x1, starting transfers between devices: none -> 7.41 us  [all_to_all(jnp.stack([arr for _ in range(axis_size(across))], axis=0), ac...]
    dot_general x1, matrix products: 17.9 us -> 24.1 us  [shards(): lax.dot_general(dy_full, _link_page(down_weight, 'dp'), (((1,), (1,)), ((...]
  transfers between devices with their start and end apart: 3 -> 3, of which waited for: 3 -> 2; matrix products, arithmetic and copies ran while one was open for 6% -> 15% of each run, Pallas kernels for 0% -> 0%
where the time goes in v1:
time: 457 us; the launch traced here: 456 us
  waiting for transfers between devices  198 us (43%)
  blocking collectives  98 us (21%)
  local copies, waits for them, and re-layouts  66.3 us (15%)
  matrix products  41.5 us (9%)
  starting transfers between devices  36.8 us (8%)
  between operations  14.4 us (3%)
    all_to_all x1, waiting for transfers between devices, all_to_all(jnp.stack([arr for _ in range(axis_size(across))], axis=0), ac...  168 us
    psum x1, blocking collectives, shards(): lax.psum((partials[0], partials[1], partials[2], partials[3]), 'tensor')  50.1 us
    psum x1, blocking collectives, shards(): lax.psum((adapter_scale_factor * apply_projection(gate_gradient_total, ga...  47.8 us
    reshape x2, local copies, waits for them, and re-layouts, jnp.concatenate(all_to_all(jnp.stack([arr for _ in range(axis_size(across...  39 us
    all_to_all x1, starting transfers between devices, shards(): lax.all_to_all(outgoing.astype(jnp.bfloat16), 'dp', split_axis=0, concat_...  29.3 us
    all_to_all x1, waiting for transfers between devices, shards(): lax.all_to_all(outgoing.astype(jnp.bfloat16), 'dp', split_axis=0, concat_...  29.1 us
    dot_general x1, matrix products, shards(): lax.dot_general(dy_full, _link_page(down_weight, 'dp'), (((1,), (1,)), ((...  24.1 us
  transfers between devices with their start and end apart: 3, of which 2 were waited for; matrix products, arithmetic and copies ran while one was open for 15% of the time, Pallas kernels for 0%

profile of v1, /device:TPU:112, one launch (start us, length us, event | category | flops | bytes accessed | tf_op | source)
XLA Modules:
  0.0 455.7 jit_solution(3300854580797842740)
XLA Ops:
  7.9 7.7 %stack.2 = bf16[16,896,512]{2,1,0:T(8,128)(2,1)} broadcast(bf16[896,512]{1,0:T(8,128)(2,1)} %param.21), dimensions={1,2} | broadcast | bytes 15597568 | tf_op jit(solution)/shard_map/stack | solution.py:9
  15.7 7.4 %all-to-all-start = ((bf16[16,896,512]{2,1,0:T(8,128)(2,1)}), bf16[16,896,512]{2,1,0:T(8,128)(2,1)}, u32[]{:S(2)}, u32[]{:S(2)}) async-start(bf16[16,896,512]{2,1,0:T(8,128)(2,1)} %stack.2), calls=%async_computation | async-start | bytes 29360128 | tf_op jit(solution)/shard_map/all_to_all | solution.py:9
  23.4 1.7 gather_fusion.2
  25.7 2.0 gather_fusion.5
  27.7 1.9 gather_fusion.1
  29.6 1.7 gather_fusion.4
  32.9 1.8 gather_fusion.6
  35.9 1.2 gather_fusion
  39.3 50.1 %psum.42 = bf16[6,16,128]{2,1,0:T(8,128)(2,1)S(1)} all-reduce(f32[6,16,128]{2,1,0:T(8,128)S(1)} %fusion.23), channel_id=1, replica_groups=mesh['dp'=16,'tensor'=16] {'tensor'}, use_global_device_ids=true, to_apply=%region_0.0 | all-reduce | flops 12288 | bytes 73728 | tf_op jit(solution)/shard_map/psum | solution.py:64
  89.4 2.1 fusion.29
  91.6 167.9 %all-to-all-done = bf16[16,896,512]{2,1,0:T(8,128)(2,1)} async-done(((bf16[16,896,512]{2,1,0:T(8,128)(2,1)}), bf16[16,896,512]{2,1,0:T(8,128)(2,1)}, u32[]{:S(2)}, u32[]{:S(2)}) %all-to-all-start) | async-done | bytes 14680096 | tf_op jit(solution)/shard_map/all_to_all | solution.py:9
  259.5 16.5 %copy.56 = bf16[896,16,512]{2,1,0:T(8,128)(2,1)} copy(bf16[896,16,512]{2,0,1:T(8,128)(2,1)} %bitcast.2) | data formatting | bytes 29360128 | tf_op jit(solution)/shard_map/reshape | solution.py:8
  276.0 22.5 %reshape.345 = bf16[896,8192,1]{1,0,2:T(8,128)(2,1)} reshape(bf16[896,16,512]{2,1,0:T(8,128)(2,1)} %copy.56) | data formatting | bytes 29360128 | tf_op jit(solution)/shard_map/reshape | solution.py:8
  298.5 24.1 %fusion.10 = (bf16[6,128,896]{2,1,0:T(8,128)(2,1)}, bf16[6,128,896]{2,1,0:T(8,128)(2,1)}, bf16[6,128,896]{2,1,0:T(8,128)(2,1)S(1)}) fusion(bf16[6,128,896]{2,1,0:T(8,128)(2,1)} %bitcast.58, bf16[6,128,896]{2,1,0:T(8,128)(2,1)} %bitcast.59, f32[6,128,896]{2,1,0:T(8,128)} %fusion.29, bf16[6,128,8192]{2,1,0:T(8,128)(2,1)} %bitcast.57, ...), kind=kOutput, calls=%fused_computation.24 | convolution fusion | flops 11288051712 | bytes 36896768 | tf_op jit(solution)/shard_map/dot_general | solution.py:70
  322.7 2.6 convolution_multiply_fusion.4
  325.3 1.2 convolution_multiply_fusion.5
  327.3 47.8 %all-reduce.2 = (bf16[6,16,128]{2,1,0:T(8,128)(2,1)S(1)}, bf16[6,16,128]{2,1,0:T(8,128)(2,1)S(1)}, bf16[6,16,128]{2,1,0:T(8,128)(2,1)S(1)}, bf16[6,16,128]{2,1,0:T(8,128)(2,1)S(1)}, bf16[6,16,128]{2,1,0:T(8,128)(2,1)S(1)}) all-reduce(f32[6,16,128]{2,1,0:T(8,128)S(1)} %copy-done.15, ...), channel_id=1, replica_groups=mesh['dp'=16,'tensor'=16] {'tensor'}, use_global_device_ids=true, to_apply=%region_1.4 | all-reduce | flops 61440 | bytes 368640 | tf_op jit(solution)/shard_map/psum | solution.py:86
  375.4 1.8 fusion.17
  378.4 2.6 fusion
  381.0 1.7 copy.62
  382.8 29.3 %all-to-all-start.1 = ((bf16[16,1,16,4224]{3,2,1,0:T(8,128)(2,1)}), bf16[16,1,16,4224]{3,2,1,0:T(8,128)(2,1)S(1)}, u32[]{:S(2)}, u32[]{:S(2)}) async-start(bf16[16,1,16,4224]{3,2,1,0:T(8,128)(2,1)} %copy.62), calls=%async_computation.1 | async-start | bytes 4325376 | tf_op jit(solution)/shard_map/all_to_all | solution.py:140
  413.0 1.3 add_convert_fusion
  414.3 29.1 %all-to-all-done.1 = bf16[16,1,16,4224]{3,2,1,0:T(8,128)(2,1)S(1)} async-done(((bf16[16,1,16,4224]{3,2,1,0:T(8,128)(2,1)}), bf16[16,1,16,4224]{3,2,1,0:T(8,128)(2,1)S(1)}, u32[]{:S(2)}, u32[]{:S(2)}) %all-to-all-start.1) | async-done | bytes 2162720 | tf_op jit(solution)/shard_map/all_to_all | solution.py:140
  443.4 1.1 fusion.11
  (88 shorter events, 13.9 us)
Async XLA Ops:
  7.2 17.9 %copy-start = (bf16[48,16,896]{2,1,0:T(8,128)(2,1)S(1)}, bf16[48,16,896]{2,1,0:T(8,128)(2,1)}, u32[]{:S(2)}) copy-start(bf16[48,16,896]{2,1,0:T(8,128)(2,1)} %param.26) | copy-start | bytes 4128772
  7.2 291.4 %all-gather.2.cloned.1.call-start = ((), (), s32[]{:S(2)}) async-start(), calls=%async_computation.2 | async-start | bytes 13369344 | tf_op jit(solution)/shard_map/all_gather | solution.py:69
  15.7 7.4 %copy-start.22 = (s32[96]{0:T(128)S(1)}, s32[96]{0:T(128)}, u32[]{:S(2)}) copy-start(s32[96]{0:T(128)} %param.28) | copy-start | bytes 1156
  15.7 16.3 %copy-start.2 = (bf16[768,512]{1,0:T(8,128)(2,1)S(1)}, bf16[768,512]{1,0:T(8,128)(2,1)}, u32[]{:S(2)}) copy-start(bf16[768,512]{1,0:T(8,128)(2,1)} %param.18) | copy-start | bytes 2359300
  15.7 243.8 %all-to-all-start = ((bf16[16,896,512]{2,1,0:T(8,128)(2,1)}), bf16[16,896,512]{2,1,0:T(8,128)(2,1)}, u32[]{:S(2)}, u32[]{:S(2)}) async-start(bf16[16,896,512]{2,1,0:T(8,128)(2,1)} %stack.2), calls=%async_computation | async-start | bytes 29360128 | tf_op jit(solution)/shard_map/all_to_all | solution.py:9
  25.1 10.7 %copy-start.23 = (s32[48]{0:T(128)S(1)}, s32[48]{0:T(128)}, u32[]{:S(2)}) copy-start(s32[48]{0:T(128)} %param.29) | copy-start | bytes 580
  25.7 63.8 %copy-start.6 = (bf16[6,16,896]{2,1,0:T(8,128)(2,1)}, bf16[6,16,896]{2,1,0:T(8,128)(2,1)S(1)}, u32[]{:S(2)}) copy-start(bf16[6,16,896]{2,1,0:T(8,128)(2,1)S(1)} %gather_fusion.3) | copy-start | bytes 516100
  34.7 1.1 copy-start.8
  35.9 3.0 copy-start.3
  322.7 2.7 copy-start.5
  322.7 3.9 copy-start.7
  325.3 1.8 copy-start.12
  325.3 1.8 copy-start.13
  325.3 1.8 copy-start.14
  326.5 0.8 copy-start.15
  375.2 2.2 copy-start.16
  375.2 2.2 copy-start.18
  375.4 2.0 copy-start.4
  382.8 29.4 %copy-start.11 = (bf16[6,16,512]{2,1,0:T(8,128)(2,1)S(1)}, bf16[6,16,512]{2,1,0:T(8,128)(2,1)}, u32[]{:S(2)}) copy-start(bf16[6,16,512]{2,1,0:T(8,128)(2,1)} %copy-done.10) | copy-start | bytes 294916
  382.8 29.4 %copy-start.19 = (bf16[6,16,128]{2,1,0:T(8,128)(2,1)S(1)}, bf16[6,16,128]{2,1,0:T(8,128)(2,1)}, u32[]{:S(2)}) copy-start(bf16[6,16,128]{2,1,0:T(8,128)(2,1)} %copy-done.18) | copy-start | bytes 73732
  382.8 60.7 %all-to-all-start.1 = ((bf16[16,1,16,4224]{3,2,1,0:T(8,128)(2,1)}), bf16[16,1,16,4224]{3,2,1,0:T(8,128)(2,1)S(1)}, u32[]{:S(2)}, u32[]{:S(2)}) async-start(bf16[16,1,16,4224]{3,2,1,0:T(8,128)(2,1)} %copy.62), calls=%async_computation.1 | async-start | bytes 4325376 | tf_op jit(solution)/shard_map/all_to_all | solution.py:140
  412.1 0.9 copy-start.9
  412.1 0.9 copy-start.17
  444.5 4.3 copy-start.1
  (3 other events, 2.0 us)
Sparse Core Ops, SparseCore 0:
  9.8 77.1 all-gather.1
